TPU v7x, 256 devices: a whole 4x4x8 slice. The times are simulated.
256 devices in a mesh: dp: 4 (over z_hi), mx: 8 (over z_lo, y), my: 8 (over x, core).
Axes of the slice: x: 4, y: 4, z: 8 (z_hi: 4, z_lo: 2; z = z_hi * 2 + z_lo), core: 2. Of those that a mesh axis runs over, the one named last changes fastest.
Arguments:
- inputs: bfloat16 [768, 4096], P(('dp', 'mx', 'my')), may hold values from -6 to 6
- weight_means: bfloat16 [3, 14336, 4096], P(None, ('mx', 'my'), 'dp'), may hold values from -6 to 6
- weight_sigmas: bfloat16 [3, 14336, 4096], P(None, ('mx', 'my'), 'dp'), may hold values from 0.099609375 to 1
- weight_noise: bfloat16 [3, 14336, 4096], P(None, ('mx', 'my'), 'dp'), may hold values from -6 to 6
- input_signs: int32 [768, 4096], P(('dp', 'mx', 'my')), may hold values 0 or 1
- output_signs: int32 [2, 14336, 768], P(None, ('mx', 'my'), 'dp'), may hold values 0 or 1
- hidden_signs: int32 [14336, 768], P(('mx', 'my'), 'dp'), may hold values 0 or 1
- result_signs: int32 [768, 4096], P(('dp', 'mx', 'my')), may hold values 0 or 1
- cotangent: bfloat16 [768, 4096], P(('dp', 'mx', 'my')), may hold values from -6 to 6
Outputs:
- result: bfloat16 [768, 4096], P(('dp', 'mx', 'my'))
- input_grad: bfloat16 [768, 4096], P(('dp', 'mx', 'my'))
- mean_grad: bfloat16 [3, 14336, 4096], P(None, ('mx', 'my'), 'dp')
- sigma_grad: bfloat16 [3, 14336, 4096], P(None, ('mx', 'my'), 'dp')
All inputs are finite; a program needn't handle non-finite values. No bound on the sum of `input_signs` or of `output_signs` or of `hidden_signs` or of `result_signs` on one device may be relied on, other than what follows from the above.
Results may differ from a plain program's by a relative error of at most 0.02.
Values may be sent and summed in bfloat16 or wider, within the bound.
No kernel may reach another device: no remote copies, remote signals or barrier semaphores. Data moves between devices by JAX's collectives and lax.ppermute only.
A program may use at most 128 MiB of HBM per device.

v0:
```python
import jax
import jax.numpy as jnp
from jax import lax
from jax.sharding import PartitionSpec as P

D = 4096
FF = 14336


def sent_together(arrays, axis, dim, along):
    both = jnp.concatenate(arrays, axis=along)
    out, at, gathered = (lax.all_gather(both, axis, axis=dim, tiled=True), 0, [])
    for a in arrays:
        gathered.append(lax.slice_in_dim(out, at, at + a.shape[along], axis=along))
        at += a.shape[along]
    return tuple(gathered)


def cut_along(x, dim, size):
    before, after = (x.shape[:dim], x.shape[dim + 1 :])
    return jnp.moveaxis(x.reshape(*before, size, -1, *after), dim, 0)


def sent_and_summed(x, axis, dim):
    tiles = cut_along(x, dim, lax.axis_size(axis))
    arrived = lax.all_to_all(tiles, axis, split_axis=0, concat_axis=0, tiled=True)
    return arrived.astype(jnp.float32).sum(axis=0)


def side_by_side(arrays, axis, dim, along):
    widths = [a.shape[along] for a in arrays]
    both = jnp.concatenate(arrays, axis=along)
    out = sent_and_summed(both, axis, dim)
    return tuple(jnp.split(out, [sum(widths[:k]) for k in range(1, len(widths))], axis=along))


def laid_out(tiles, dim):
    lengths = list(tiles.shape[1:])
    lengths[dim] *= tiles.shape[0]
    return jnp.moveaxis(tiles, 0, dim).reshape(lengths)


def from_everyone(x, axis):
    size = lax.axis_size(axis)
    return lax.all_to_all(jnp.broadcast_to(x[None], (size, *x.shape)), axis, 0, 0, tiled=True)


def collect(x, axis, dim):
    return laid_out(from_everyone(x, axis), dim)


def side_by_side_2(arrays, axis, dim, along):
    widths = [a.shape[along] for a in arrays]
    both = jnp.concatenate(arrays, axis=along)
    out = collect(both, axis, dim)
    return tuple(jnp.split(out, [sum(widths[:k]) for k in range(1, len(widths))], axis=along))


def in_one_piece(arrays, axis, split_dim, concat_dim, along):
    ends, at = ([], 0)
    for a in arrays[:-1]:
        at += a.shape[along]
        ends.append(at)
    both = jnp.concatenate(arrays, axis=along)
    return tuple(
        jnp.split(
            lax.all_to_all(both, axis, split_axis=split_dim, concat_axis=concat_dim, tiled=True),
            ends,
            axis=along,
        )
    )


def to_sign(values):
    return (2 * values - 1).astype(jnp.float32)


def left_trans(left, right):
    return lax.dot_general(
        left, right, (((0,), (0,)), ((), ())), preferred_element_type=jnp.float32
    )


def right_trans(left, right):
    return lax.dot_general(
        left, right, (((1,), (1,)), ((), ())), preferred_element_type=jnp.float32
    )


def group_sum(left, right, groups, scale):
    left_groups = left.reshape(left.shape[0], groups, -1)
    right_groups = right.reshape(groups, -1, right.shape[1])
    terms = scale * jnp.einsum(
        "fgt,gtd->gfd", left_groups, right_groups, preferred_element_type=jnp.float32
    )
    rounded = lax.optimization_barrier(terms.astype(jnp.bfloat16))
    return jnp.sum(rounded.astype(jnp.float32), axis=0)


def on_device(
    inputs,
    weight_means,
    weight_sigmas,
    weight_noise,
    input_signs,
    output_signs,
    hidden_signs,
    result_signs,
    cotangent,
):
    scale_in = D ** (-0.5)
    scale_out = FF ** (-0.5)
    in_flip = to_sign(input_signs)
    out_flip = to_sign(output_signs)
    hid_flip = to_sign(hidden_signs)
    res_flip = to_sign(result_signs)
    perturb = (weight_sigmas.astype(jnp.float32) * weight_noise.astype(jnp.float32)).astype(
        jnp.bfloat16
    )
    flipped = (inputs.astype(jnp.float32) * in_flip).astype(jnp.bfloat16)
    all_inputs, all_flipped = sent_together((inputs, flipped), ("mx", "my"), 0, 1)
    groups = lax.axis_size("dp")
    tok_rows = all_inputs.shape[0]
    block_inputs, block_flipped = (
        lax.all_to_all(all_inputs, "dp", split_axis=1, concat_axis=0, tiled=True),
        lax.all_to_all(all_flipped, "dp", split_axis=1, concat_axis=0, tiled=True),
    )
    mean_part = jnp.stack(
        [
            scale_in * right_trans(weight_means[0], block_inputs),
            scale_in * right_trans(weight_means[1], block_inputs),
        ]
    )
    pert_part = jnp.stack(
        [
            scale_in * right_trans(perturb[0], block_flipped),
            scale_in * right_trans(perturb[1], block_flipped),
        ]
    )
    mean_part, pert_part = side_by_side(
        (mean_part.astype(jnp.bfloat16), pert_part.astype(jnp.bfloat16)), "dp", 2, 0
    )
    gate = mean_part[0] + pert_part[0] * out_flip[0]
    up = mean_part[1] + pert_part[1] * out_flip[1]
    gate_sig = jax.nn.sigmoid(gate)
    hidden = (gate * gate_sig * up).astype(jnp.bfloat16)
    hid_flipped = (hidden.astype(jnp.float32) * hid_flip).astype(jnp.bfloat16)
    all_hidden, all_hid_flipped = side_by_side_2((hidden, hid_flipped), "dp", 1, 0)
    res_mean = (scale_out * left_trans(all_hidden, weight_means[2])).reshape(groups, tok_rows, -1)
    res_pert = (scale_out * left_trans(all_hid_flipped, perturb[2])).reshape(groups, tok_rows, -1)
    res_mean, res_pert = side_by_side(
        (res_mean.astype(jnp.bfloat16), res_pert.astype(jnp.bfloat16)), ("mx", "my"), 1, 0
    )
    res_mean, res_pert = tuple(
        (
            part.astype(jnp.float32)
            for part in in_one_piece(
                (res_mean.astype(jnp.bfloat16), res_pert.astype(jnp.bfloat16)), "dp", 0, 2, 1
            )
        )
    )
    result = (res_mean[0] + res_pert[0] * res_flip).astype(jnp.bfloat16)
    cot_flipped = (cotangent.astype(jnp.float32) * res_flip).astype(jnp.bfloat16)
    all_cot, all_cot_flipped = sent_together((cotangent, cot_flipped), ("mx", "my"), 0, 1)
    block_cot, block_cot_flipped = (
        lax.all_to_all(all_cot, "dp", split_axis=1, concat_axis=0, tiled=True),
        lax.all_to_all(all_cot_flipped, "dp", split_axis=1, concat_axis=0, tiled=True),
    )
    hid_mean = scale_out * right_trans(weight_means[2], block_cot)
    hid_pert = scale_out * right_trans(perturb[2], block_cot_flipped)
    hid_mean, hid_pert = side_by_side(
        (hid_mean.astype(jnp.bfloat16), hid_pert.astype(jnp.bfloat16)), "dp", 1, 0
    )
    hid_grad = hid_mean + hid_pert * hid_flip
    up_grad = (hid_grad * gate * gate_sig).astype(jnp.bfloat16)
    gate_grad = (hid_grad * up * gate_sig * (1.0 + gate * (1.0 - gate_sig))).astype(jnp.bfloat16)
    gate_flipped = (gate_grad.astype(jnp.float32) * out_flip[0]).astype(jnp.bfloat16)
    up_flipped = (up_grad.astype(jnp.float32) * out_flip[1]).astype(jnp.bfloat16)
    gate_rows, up_rows, gate_frows, up_frows = side_by_side_2(
        (gate_grad, up_grad, gate_flipped, up_flipped), "dp", 1, 0
    )
    mean_total = jnp.stack(
        [
            group_sum(gate_rows, block_inputs, groups, scale_in),
            group_sum(up_rows, block_inputs, groups, scale_in),
            group_sum(all_hidden, block_cot, groups, scale_out),
        ]
    )
    pert_total = jnp.stack(
        [
            group_sum(gate_frows, block_flipped, groups, scale_in),
            group_sum(up_frows, block_flipped, groups, scale_in),
            group_sum(all_hid_flipped, block_cot_flipped, groups, scale_out),
        ]
    )
    back_mean = scale_in * (
        left_trans(gate_rows, weight_means[0]) + left_trans(up_rows, weight_means[1])
    )
    back_pert = scale_in * (left_trans(gate_frows, perturb[0]) + left_trans(up_frows, perturb[1]))
    back_mean = back_mean.reshape(groups, tok_rows, -1)
    back_pert = back_pert.reshape(groups, tok_rows, -1)
    back_mean, back_pert = side_by_side(
        (back_mean.astype(jnp.bfloat16), back_pert.astype(jnp.bfloat16)), ("mx", "my"), 1, 0
    )
    back_mean, back_pert = tuple(
        (
            part.astype(jnp.float32)
            for part in in_one_piece(
                (back_mean.astype(jnp.bfloat16), back_pert.astype(jnp.bfloat16)), "dp", 0, 2, 1
            )
        )
    )
    input_grad = (back_mean[0] + back_pert[0] * in_flip).astype(jnp.bfloat16)
    mean_grad = mean_total.astype(jnp.bfloat16)
    sigma_grad = (pert_total * weight_noise.astype(jnp.float32)).astype(jnp.bfloat16)
    return (result, input_grad, mean_grad, sigma_grad)


def solution(mesh):
    return jax.shard_map(
        on_device,
        mesh=mesh,
        in_specs=(
            P(("dp", "mx", "my"), None),
            P(None, ("mx", "my"), "dp"),
            P(None, ("mx", "my"), "dp"),
            P(None, ("mx", "my"), "dp"),
            P(("dp", "mx", "my"), None),
            P(None, ("mx", "my"), "dp"),
            P(("mx", "my"), "dp"),
            P(("dp", "mx", "my"), None),
            P(("dp", "mx", "my"), None),
        ),
        out_specs=(
            P(("dp", "mx", "my"), None),
            P(("dp", "mx", "my"), None),
            P(None, ("mx", "my"), "dp"),
            P(None, ("mx", "my"), "dp"),
        ),
        check_vma=False,
    )
```

profile of v0, /device:TPU:8, one launch (start us, length us, event | category | flops | bytes accessed | tf_op | source)
XLA Modules:
  0.0 650.1 jit_solution(4601174362694766621)
XLA Ops:
  8.1 1.4 maximum_bitcast_fusion.3
  10.5 1.4 maximum_bitcast_fusion.4
  11.9 108.3 %all-gather.5.cloned.1.call-done = bf16[64,3,8192]{2,1,0:T(4,128)(2,1)} async-done(((bf16[1,3,8192]{2,1,0:T(4,128)(2,1)}), bf16[64,3,8192]{2,1,0:T(4,128)(2,1)}) %all-gather.5.cloned.1.call-update) | async-done | bytes 3145744 | tf_op jit(solution)/shard_map/all_gather | solution.py:12
  120.3 7.5 %reshape.94 = bf16[192,8192]{1,0:T(8,128)(2,1)} reshape(bf16[64,3,8192]{2,1,0:T(4,128)(2,1)} %all-gather.5.cloned.1.call-done) | data formatting | bytes 6291456
  127.8 3.4 fusion.48
  132.5 6.6 %all-to-all-start.1 = ((bf16[192,4,1024]{2,0,1:T(8,128)(2,1)}), bf16[192,4,1024]{2,0,1:T(8,128)(2,1)S(1)}, u32[]{:S(2)}, u32[]{:S(2)}) async-start(bf16[192,4,1024]{2,0,1:T(8,128)(2,1)} %bitcast.197), calls=%async_computation.1 | async-start | bytes 3145728 | tf_op jit(solution)/shard_map/all_to_all | solution.py:126
  139.1 98.6 %all-gather.7.cloned.1.call-done = bf16[64,3,8192]{2,1,0:T(4,128)(2,1)} async-done(((bf16[1,3,8192]{2,1,0:T(4,128)(2,1)}), bf16[64,3,8192]{2,1,0:T(4,128)(2,1)}) %all-gather.7.cloned.1.call-update) | async-done | bytes 3145744 | tf_op jit(solution)/shard_map/all_gather | solution.py:12
  237.7 7.4 %reshape.96 = bf16[192,8192]{1,0:T(8,128)(2,1)} reshape(bf16[64,3,8192]{2,1,0:T(4,128)(2,1)} %all-gather.7.cloned.1.call-done) | data formatting | bytes 6291456
  245.1 3.4 fusion.47
  249.8 5.9 all-to-all-start.7
  255.7 2.8 copy.51
  258.4 34.4 %all-to-all-done.7 = bf16[192,4,1024]{2,0,1:T(8,128)(2,1)S(1)} async-done(((bf16[192,4,1024]{2,0,1:T(8,128)(2,1)}), bf16[192,4,1024]{2,0,1:T(8,128)(2,1)S(1)}, u32[]{:S(2)}, u32[]{:S(2)}) %all-to-all-start.7) | async-done | bytes 1572896 | tf_op jit(solution)/shard_map/all_to_all | solution.py:167
  292.8 5.2 all-to-all-start.6
  298.0 2.7 copy.53
  300.7 40.0 %all-to-all-done.6 = bf16[192,4,1024]{2,0,1:T(8,128)(2,1)} async-done(((bf16[192,4,1024]{2,0,1:T(8,128)(2,1)}), bf16[192,4,1024]{2,0,1:T(8,128)(2,1)}, u32[]{:S(2)}, u32[]{:S(2)}) %all-to-all-start.6) | async-done | bytes 1572896 | tf_op jit(solution)/shard_map/all_to_all | solution.py:166
  340.6 4.5 all-to-all-start
  345.2 2.3 fusion
  348.2 2.2 fusion.14
  351.3 2.4 copy.33
  353.6 24.3 %all-to-all-done = bf16[192,4,1024]{2,0,1:T(8,128)(2,1)} async-done(((bf16[192,4,1024]{2,0,1:T(8,128)(2,1)}), bf16[192,4,1024]{2,0,1:T(8,128)(2,1)}, u32[]{:S(2)}, u32[]{:S(2)}) %all-to-all-start) | async-done | bytes 1572896 | tf_op jit(solution)/shard_map/all_to_all | solution.py:125
  377.9 4.2 all-to-all-start.8
  382.1 1.4 fusion.10
  387.2 2.1 fusion.16
  389.6 2.9 fusion.15
  395.3 3.5 all-to-all-done.8
  398.8 20.2 %all-to-all-start.2 = ((bf16[4,4,224,192]{2,3,1,0:T(8,128)(2,1)}), bf16[4,4,224,192]{2,3,1,0:T(8,128)(2,1)S(1)}, u32[]{:S(2)}, u32[]{:S(2)}) async-start(bf16[4,4,224,192]{2,3,1,0:T(8,128)(2,1)} %copy.28), calls=%async_computation.2 | async-start | bytes 3145728 | tf_op jit(solution)/shard_map/all_to_all | solution.py:26
  421.1 21.7 %all-to-all-done.2 = bf16[4,4,224,192]{2,3,1,0:T(8,128)(2,1)S(1)} async-done(((bf16[4,4,224,192]{2,3,1,0:T(8,128)(2,1)}), bf16[4,4,224,192]{2,3,1,0:T(8,128)(2,1)S(1)}, u32[]{:S(2)}, u32[]{:S(2)}) %all-to-all-start.2) | async-done | bytes 1376288 | tf_op jit(solution)/shard_map/all_to_all | solution.py:26
  445.9 11.9 %all-to-all-start.3 = ((bf16[4,448,192]{1,2,0:T(8,128)(2,1)}), bf16[4,448,192]{1,2,0:T(8,128)(2,1)S(1)}, u32[]{:S(2)}, u32[]{:S(2)}) async-start(bf16[4,448,192]{1,2,0:T(8,128)(2,1)} %broadcast_in_dim.4), calls=%async_computation.3 | async-start | bytes 1572864 | tf_op jit(solution)/shard_map/all_to_all | solution.py:45
  458.0 19.6 %all-to-all-done.3 = bf16[4,448,192]{1,2,0:T(8,128)(2,1)S(1)} async-done(((bf16[4,448,192]{1,2,0:T(8,128)(2,1)}), bf16[4,448,192]{1,2,0:T(8,128)(2,1)S(1)}, u32[]{:S(2)}, u32[]{:S(2)}) %all-to-all-start.3) | async-done | bytes 688160 | tf_op jit(solution)/shard_map/all_to_all | solution.py:45
  478.9 3.8 all-to-all-start.9
  484.1 2.8 multiply_convert_fusion.8
  486.9 5.2 convert_element_type.183
  492.0 2.8 multiply_convert_fusion.9
  494.8 5.2 convert_element_type.181
  500.0 4.9 maximum_bitcast_fusion
  504.9 5.0 copy.29
  510.0 13.6 %all-to-all-start.4 = ((bf16[64,8,3,1024]{3,1,2,0:T(8,128)(2,1)}), bf16[64,8,3,1024]{3,1,2,0:T(8,128)(2,1)}, u32[]{:S(2)}, u32[]{:S(2)}) async-start(bf16[64,8,3,1024]{3,1,2,0:T(8,128)(2,1)} %copy.29), calls=%async_computation.4 | async-start | bytes 6291456 | tf_op jit(solution)/shard_map/all_to_all | solution.py:26
  525.5 1.7 multiply_convert_fusion.7
  527.2 5.2 convert_element_type.200
  532.4 1.7 fusion.24
  534.1 2.8 multiply_convert_fusion.6
  536.9 5.2 convert_element_type.202
  542.1 4.9 maximum_bitcast_fusion.1
  547.0 5.0 copy.34
  552.0 13.5 %all-to-all-done.4 = bf16[64,8,3,1024]{3,1,2,0:T(8,128)(2,1)} async-done(((bf16[64,8,3,1024]{3,1,2,0:T(8,128)(2,1)}), bf16[64,8,3,1024]{3,1,2,0:T(8,128)(2,1)}, u32[]{:S(2)}, u32[]{:S(2)}) %all-to-all-start.4) | async-done | bytes 3145760 | tf_op jit(solution)/shard_map/all_to_all | solution.py:26
  565.5 7.8 %all-to-all-start.10 = ((bf16[64,8,3,1024]{3,1,2,0:T(8,128)(2,1)}), bf16[64,8,3,1024]{3,1,2,0:T(8,128)(2,1)}, u32[]{:S(2)}, u32[]{:S(2)}) async-start(bf16[64,8,3,1024]{3,1,2,0:T(8,128)(2,1)} %copy.34), calls=%async_computation.10 | async-start | bytes 6291456 | tf_op jit(solution)/shard_map/all_to_all | solution.py:26
  573.4 3.8 multiply_convert_fusion
  577.2 3.4 multiply_convert_fusion.3
  580.5 1.9 reduce.4
  582.4 2.8 convert_reduce_fusion
  585.3 2.2 multiply_convert_fusion.2
  587.4 2.2 multiply_convert_fusion.1
  589.6 3.4 multiply_convert_fusion.5
  592.9 1.9 reduce.2
  594.8 3.6 multiply_convert_fusion.4
  598.4 1.9 reduce.3
  605.3 1.6 fusion.1
  607.0 2.4 reduce
  610.1 5.1 all-to-all-done.10
  615.2 7.2 %all-to-all-start.5 = ((bf16[4,6,1024]{2,1,0:T(8,128)(2,1)}), bf16[4,6,1024]{2,1,0:T(8,128)(2,1)S(1)}, u32[]{:S(2)}, u32[]{:S(2)}) async-start(bf16[4,6,1024]{2,1,0:T(8,128)(2,1)} %pad_maximum_fusion.4), calls=%async_computation.5 | async-start | bytes 131072 | tf_op jit(solution)/shard_map/all_to_all | solution.py:67
  622.5 2.5 reduce.1
  625.7 5.0 all-to-all-done.5
  630.7 3.3 all-to-all-start.11
  634.6 7.5 %all-to-all-done.11 = bf16[4,6,1024]{2,1,0:T(8,128)(2,1)S(1)} async-done(((bf16[4,6,1024]{2,1,0:T(8,128)(2,1)}), bf16[4,6,1024]{2,1,0:T(8,128)(2,1)S(1)}, u32[]{:S(2)}, u32[]{:S(2)}) %all-to-all-start.11) | async-done | bytes 49184 | tf_op jit(solution)/shard_map/all_to_all | solution.py:67
  (78 shorter events, 30.6 us)
Async XLA Ops:
  7.2 113.1 %all-gather.5.cloned.1.call-start = ((), (), s32[]{:S(2)}) async-start(), calls=%async_computation.12 | async-start | bytes 4259840 | tf_op jit(solution)/shard_map/all_gather | solution.py:12
  9.6 228.1 %all-gather.7.cloned.1.call-start = ((), (), s32[]{:S(2)}) async-start(), calls=%async_computation.13 | async-start | bytes 4259840 | tf_op jit(solution)/shard_map/all_gather | solution.py:12
  132.5 117.3 %all-to-all-start.1 = ((bf16[192,4,1024]{2,0,1:T(8,128)(2,1)}), bf16[192,4,1024]{2,0,1:T(8,128)(2,1)S(1)}, u32[]{:S(2)}, u32[]{:S(2)}) async-start(bf16[192,4,1024]{2,0,1:T(8,128)(2,1)} %bitcast.197), calls=%async_computation.1 | async-start | bytes 3145728 | tf_op jit(solution)/shard_map/all_to_all | solution.py:126
  249.8 43.0 %all-to-all-start.7 = ((bf16[192,4,1024]{2,0,1:T(8,128)(2,1)}), bf16[192,4,1024]{2,0,1:T(8,128)(2,1)S(1)}, u32[]{:S(2)}, u32[]{:S(2)}) async-start(bf16[192,4,1024]{2,0,1:T(8,128)(2,1)} %bitcast.195), calls=%async_computation.7 | async-start | bytes 3145728 | tf_op jit(solution)/shard_map/all_to_all | solution.py:167
  292.8 54.7 %copy-start.4 = (bf16[192,4,1024]{2,0,1:T(8,128)(2,1)}, bf16[192,4,1024]{2,0,1:T(8,128)(2,1)S(1)}, u32[]{:S(2)}) copy-start(bf16[192,4,1024]{2,0,1:T(8,128)(2,1)S(1)} %all-to-all-done.7) | copy-start | bytes 4718596
  292.8 47.9 %all-to-all-start.6 = ((bf16[192,4,1024]{2,0,1:T(8,128)(2,1)}), bf16[192,4,1024]{2,0,1:T(8,128)(2,1)}, u32[]{:S(2)}, u32[]{:S(2)}) async-start(bf16[192,4,1024]{2,0,1:T(8,128)(2,1)} %bitcast.196), calls=%async_computation.6 | async-start | bytes 3145728 | tf_op jit(solution)/shard_map/all_to_all | solution.py:166
  340.6 37.3 %all-to-all-start = ((bf16[192,4,1024]{2,0,1:T(8,128)(2,1)}), bf16[192,4,1024]{2,0,1:T(8,128)(2,1)}, u32[]{:S(2)}, u32[]{:S(2)}) async-start(bf16[192,4,1024]{2,0,1:T(8,128)(2,1)} %bitcast.198), calls=%async_computation | async-start | bytes 3145728 | tf_op jit(solution)/shard_map/all_to_all | solution.py:125
  347.5 2.8 copy-start.6
  351.3 30.9 %copy-start.7 = (bf16[3,224,1024]{2,1,0:T(8,128)(2,1)S(1)}, bf16[3,224,1024]{2,1,0:T(8,128)(2,1)}, u32[]{:S(2)}) copy-start(bf16[3,224,1024]{2,1,0:T(8,128)(2,1)} %copy-done.6) | copy-start | bytes 4128772
  377.9 20.9 %all-to-all-start.8 = ((bf16[4,448,192]{1,2,0:T(8,128)(2,1)}), bf16[4,448,192]{1,2,0:T(8,128)(2,1)}, u32[]{:S(2)}, u32[]{:S(2)}) async-start(bf16[4,448,192]{1,2,0:T(8,128)(2,1)} %bitcast.217), calls=%async_computation.8 | async-start | bytes 1572864 | tf_op jit(solution)/shard_map/all_to_all | solution.py:26
  395.3 23.7 %copy-start.12 = (s32[2,224,192]{1,2,0:T(8,128)S(1)}, s32[2,224,192]{1,2,0:T(8,128)}, u32[]{:S(2)}) copy-start(s32[2,224,192]{1,2,0:T(8,128)} %param.14) | copy-start | bytes 1032196
  398.8 44.0 %all-to-all-start.2 = ((bf16[4,4,224,192]{2,3,1,0:T(8,128)(2,1)}), bf16[4,4,224,192]{2,3,1,0:T(8,128)(2,1)S(1)}, u32[]{:S(2)}, u32[]{:S(2)}) async-start(bf16[4,4,224,192]{2,3,1,0:T(8,128)(2,1)} %copy.28), calls=%async_computation.2 | async-start | bytes 3145728 | tf_op jit(solution)/shard_map/all_to_all | solution.py:26
  442.8 1.0 copy-start.9
  442.8 1.0 copy-start.10
  444.9 12.9 %copy-start.13 = (bf16[224,192]{0,1:T(8,128)(2,1)S(1)}, bf16[224,192]{0,1:T(8,128)(2,1)}, u32[]{:S(2)}) copy-start(bf16[224,192]{0,1:T(8,128)(2,1)} %get-tuple-element.7) | copy-start | bytes 258052
  444.9 12.9 %copy-start.14 = (bf16[224,192]{0,1:T(8,128)(2,1)S(1)}, bf16[224,192]{0,1:T(8,128)(2,1)}, u32[]{:S(2)}) copy-start(bf16[224,192]{0,1:T(8,128)(2,1)} %get-tuple-element.8) | copy-start | bytes 258052
  445.9 31.6 %all-to-all-start.3 = ((bf16[4,448,192]{1,2,0:T(8,128)(2,1)}), bf16[4,448,192]{1,2,0:T(8,128)(2,1)S(1)}, u32[]{:S(2)}, u32[]{:S(2)}) async-start(bf16[4,448,192]{1,2,0:T(8,128)(2,1)} %broadcast_in_dim.4), calls=%async_computation.3 | async-start | bytes 1572864 | tf_op jit(solution)/shard_map/all_to_all | solution.py:45
  477.5 1.4 copy-start.2
  478.9 31.0 %all-to-all-start.9 = ((bf16[4,896,192]{1,2,0:T(8,128)(2,1)}), bf16[4,896,192]{1,2,0:T(8,128)(2,1)S(1)}, u32[]{:S(2)}, u32[]{:S(2)}) async-start(bf16[4,896,192]{1,2,0:T(8,128)(2,1)} %broadcast_in_dim.5), calls=%async_computation.9 | async-start | bytes 2752512 | tf_op jit(solution)/shard_map/all_to_all | solution.py:45
  510.0 55.5 %all-to-all-start.4 = ((bf16[64,8,3,1024]{3,1,2,0:T(8,128)(2,1)}), bf16[64,8,3,1024]{3,1,2,0:T(8,128)(2,1)}, u32[]{:S(2)}, u32[]{:S(2)}) async-start(bf16[64,8,3,1024]{3,1,2,0:T(8,128)(2,1)} %copy.29), calls=%async_computation.4 | async-start | bytes 6291456 | tf_op jit(solution)/shard_map/all_to_all | solution.py:26
  523.6 1.3 copy-start.11
  565.5 49.8 %all-to-all-start.10 = ((bf16[64,8,3,1024]{3,1,2,0:T(8,128)(2,1)}), bf16[64,8,3,1024]{3,1,2,0:T(8,128)(2,1)}, u32[]{:S(2)}, u32[]{:S(2)}) async-start(bf16[64,8,3,1024]{3,1,2,0:T(8,128)(2,1)} %copy.34), calls=%async_computation.10 | async-start | bytes 6291456 | tf_op jit(solution)/shard_map/all_to_all | solution.py:26
  573.3 3.8 copy-start.3
  600.3 2.0 copy-start.1
  602.3 1.5 copy-start
  603.8 1.3 copy-start.5
  603.8 1.6 copy-start.8
  615.2 15.4 %all-to-all-start.5 = ((bf16[4,6,1024]{2,1,0:T(8,128)(2,1)}), bf16[4,6,1024]{2,1,0:T(8,128)(2,1)S(1)}, u32[]{:S(2)}, u32[]{:S(2)}) async-start(bf16[4,6,1024]{2,1,0:T(8,128)(2,1)} %pad_maximum_fusion.4), calls=%async_computation.5 | async-start | bytes 131072 | tf_op jit(solution)/shard_map/all_to_all | solution.py:67
  622.4 11.5 %copy-start.15 = (s32[3,4096]{1,0:T(4,128)S(1)}, s32[3,4096]{1,0:T(4,128)}, u32[]{:S(2)}) copy-start(s32[3,4096]{1,0:T(4,128)} %param.16) | copy-start | bytes 147460
  622.4 19.7 %copy-start.16 = (s32[3,4096]{1,0:T(4,128)S(1)}, s32[3,4096]{1,0:T(4,128)}, u32[]{:S(2)}) copy-start(s32[3,4096]{1,0:T(4,128)} %param.13) | copy-start | bytes 147460
  630.7 11.5 %all-to-all-start.11 = ((bf16[4,6,1024]{2,1,0:T(8,128)(2,1)}), bf16[4,6,1024]{2,1,0:T(8,128)(2,1)S(1)}, u32[]{:S(2)}, u32[]{:S(2)}) async-start(bf16[4,6,1024]{2,1,0:T(8,128)(2,1)} %pad_maximum_fusion.5), calls=%async_computation.11 | async-start | bytes 131072 | tf_op jit(solution)/shard_map/all_to_all | solution.py:67
Sparse Core Ops, SparseCore 0:
  10.4 109.8 all-gather.4
  122.7 114.9 all-gather.6
where the time goes:
time: 660 us; the launch traced here: 650 us
  waiting for transfers between devices  381 us (58%)
  starting transfers between devices  94.4 us (14%)
  local copies, waits for them, and re-layouts  76.9 us (12%)
  matrix products  41.4 us (6%)
  other arithmetic  41.3 us (6%)
  between operations  14.8 us (2%)
    all_gather x2, waiting for transfers between devices, sent_together(): lax.all_gather(both, axis, axis=dim, tiled=True)  207 us
    all_to_all x4, starting transfers between devices, sent_and_summed(): lax.all_to_all(tiles, axis, split_axis=0, concat_axis=0, tiled=True)  45.9 us
    all_to_all x4, waiting for transfers between devices, sent_and_summed(): lax.all_to_all(tiles, axis, split_axis=0, concat_axis=0, tiled=True)  43.7 us
    all_to_all x1, waiting for transfers between devices, on_device(): lax.all_to_all(all_cot, 'dp', split_axis=1, concat_axis=0, tiled=True)  40 us
    all_to_all x1, waiting for transfers between devices, on_device(): lax.all_to_all(all_cot_flipped, 'dp', split_axis=1, concat_axis=0, tiled=...  34.4 us
    all_to_all x1, waiting for transfers between devices, on_device(): lax.all_to_all(all_inputs, 'dp', split_axis=1, concat_axis=0, tiled=True)  24.3 us
    all_to_all x2, waiting for transfers between devices, from_everyone(): lax.all_to_all(jnp.broadcast_to(x[None], (size, *x.shape)), axis, 0, 0, t...  19.6 us
    unnamed x40, local copies, waits for them, and re-layouts  19.2 us
  transfers between devices with their start and end apart: 14, of which 12 were waited for; matrix products, arithmetic and copies ran while one was open for 23% of the time, Pallas kernels for 0%

commit v1 on v0

v1 whole, which is shorter than its diff:
```python
import jax
import jax.numpy as jnp
from jax import lax
from jax.experimental import pallas as pl
from jax.experimental.pallas import tpu as pltpu
from jax.sharding import Mesh, PartitionSpec as P

D = 4096
FF = 14336
SCALE_IN = D ** (-0.5)
SCALE_OUT = FF ** (-0.5)
F = 224
T = 192
G = 4
PK = 336
CHIP = ("zl", "y", "x")
COLS = ("dp", "x", "c")
BF = jnp.bfloat16
F32 = jnp.float32


def a2a(x, axes):
    return lax.all_to_all(x, axes, split_axis=0, concat_axis=0, tiled=True)


def to_all(x, axes, n):
    return a2a(jnp.broadcast_to(x[None], (n, *x.shape)), axes)


def pack(v):
    rest = jnp.concatenate([v[: F // 2, 128:T], v[F // 2 :, 128:T]], axis=1)
    return jnp.concatenate([v[:, :128], rest], axis=0)


def unpack(v):
    rest = v[F:]
    return jnp.concatenate([v[:F], jnp.concatenate([rest[:, :64], rest[:, 64:]], axis=0)], axis=1)


def nt(a, b):
    return lax.dot_general(a, b, (((1,), (1,)), ((), ())), preferred_element_type=F32)


def tn(a, b):
    return lax.dot_general(a, b, (((0,), (0,)), ((), ())), preferred_element_type=F32)


def nn(a, b):
    return lax.dot_general(a, b, (((1,), (0,)), ((), ())), preferred_element_type=F32)


def rows_of(own, sib, which):
    parts = []
    for x in range(4):
        parts += [own[which, x, 0], sib[which, x, 0]]
    return jnp.concatenate(parts, axis=1)


def signed(a, b):
    return (a.astype(F32) * b.astype(F32)).astype(BF)


def weights_body(c_ref, m_ref, s_ref, n_ref, mo_ref, po_ref):
    c = c_ref[0]
    for x in range(4):
        for k in range(2):
            at = pl.multiple_of((2 * x + (c if k == 0 else 1 - c)) * 128, 128)
            to = pl.ds((2 * x + k) * 128, 128)
            mo_ref[0, :, to] = m_ref[0, :, pl.ds(at, 128)]
            po_ref[0, :, to] = signed(s_ref[0, :, pl.ds(at, 128)], n_ref[0, :, pl.ds(at, 128)])


def prepare_weights(c, means, sigmas, noise):
    spec = pl.BlockSpec((1, F, 1024), lambda i: (i, 0, 0))
    out = jax.ShapeDtypeStruct((3, F, 1024), BF)
    return pl.pallas_call(
        weights_body,
        grid=(3,),
        in_specs=[pl.BlockSpec(memory_space=pltpu.SMEM), spec, spec, spec],
        out_specs=[spec, spec],
        out_shape=[out, out],
        name="prepare_weights",
    )(c, means, sigmas, noise)


GATH = pl.BlockSpec((2, 4, 1, T, 128), lambda g: (0, 0, g, 0, 0))


def project_body(n, scale, own, sib, m_ref, p_ref, s_ref, o_ref):
    plain = rows_of(own, sib, 0)
    flip = signed(plain, rows_of(own, sib, 1))
    for k in range(n):
        mean = pack(nt(m_ref[k], plain))
        pert = pack(nt(p_ref[k], flip))
        sign = s_ref[0, k * PK : (k + 1) * PK].astype(F32)
        o_ref[0, k * PK : (k + 1) * PK] = (scale * mean + scale * pert * sign).astype(BF)


def project(own, sib, means, perturb, signs, first, n, scale, name):
    w = pl.BlockSpec((n, F, 1024), lambda g: (first // n, 0, 0))
    s = pl.BlockSpec((1, n * PK, 128), lambda g: (g, first // n, 0))
    return pl.pallas_call(
        lambda *refs: project_body(n, scale, *refs),
        grid=(G,),
        in_specs=[GATH, GATH, w, w, s],
        out_specs=pl.BlockSpec((1, n * PK, 128), lambda g: (g, 0, 0)),
        out_shape=jax.ShapeDtypeStruct((G, n * PK, 128), BF),
        name=name,
    )(own, sib, means, perturb, signs)


def pointwise_body(gu_ref, dh_ref, o_ref):
    def total(ref, k):
        v = ref[0, k * PK : (k + 1) * PK].astype(F32)
        for g in range(1, G):
            v = v + ref[g, k * PK : (k + 1) * PK].astype(F32)
        return v

    gate, up, dh = total(gu_ref, 0), total(gu_ref, 1), total(dh_ref, 0)
    sig = jax.nn.sigmoid(gate)
    o_ref[0:PK] = (gate * sig * up).astype(BF)
    o_ref[PK : 2 * PK] = (dh * up * sig * (1.0 + gate * (1.0 - sig))).astype(BF)
    o_ref[2 * PK :] = (dh * gate * sig).astype(BF)


def pointwise(gu, dh):
    return pl.pallas_call(
        pointwise_body, out_shape=jax.ShapeDtypeStruct((3 * PK, 128), BF), name="pointwise"
    )(gu, dh)


def back_body(n, first, scale, h_ref, s_ref, own, sib, m_ref, p_ref, oo_ref, os_ref):
    mean = pert = None
    for k in range(n):
        h = h_ref[0, k * PK : (k + 1) * PK]
        hb = signed(h, s_ref[0, k * PK : (k + 1) * PK])
        m, p = tn(unpack(h), m_ref[k]), tn(unpack(hb), p_ref[k])
        mean = m if mean is None else mean + m
        pert = p if pert is None else pert + p
    for x in range(4):
        for k, (o_ref, f_ref) in enumerate(((oo_ref, own), (os_ref, sib))):
            at = slice((2 * x + k) * 128, (2 * x + k + 1) * 128)
            sign = f_ref[0, x, 0].astype(F32)
            o_ref[x, 0] = (scale * mean[:, at] + scale * pert[:, at] * sign).astype(BF)


def back(h, signs, own, sib, means, perturb, first, n, scale, name):
    w = pl.BlockSpec((n, F, 1024), lambda g: (first // n, 0, 0))
    s = pl.BlockSpec((1, n * PK, 128), lambda g: (g, first // n, 0))
    hs = pl.BlockSpec((1, n * PK, 128), lambda g: (g, 0, 0))
    flip = pl.BlockSpec((1, 4, 1, T, 128), lambda g: (1, 0, g, 0, 0))
    o = pl.BlockSpec((4, 1, T, 128), lambda g: (0, g, 0, 0))
    out = jax.ShapeDtypeStruct((4, G, T, 128), BF)
    return pl.pallas_call(
        lambda *refs: back_body(n, first, scale, *refs),
        grid=(G,),
        in_specs=[hs, s, flip, flip, w, w],
        out_specs=[o, o],
        out_shape=[out, out],
        name=name,
    )(h, signs, own, sib, means, perturb)


def grads_body(c_ref, h_ref, gu_ref, s_ref, xo, xs, co, cs, n_ref, mo_ref, so_ref, lhs):
    c = c_ref[0]

    @pl.when(pl.program_id(0) == 0)
    def _():
        for g in range(G):
            for k in range(3):
                v = h_ref[g] if k == 2 else gu_ref[g, k * PK : (k + 1) * PK]
                lhs[2 * k, g] = unpack(v)
                lhs[2 * k + 1, g] = unpack(signed(v, s_ref[g, k * PK : (k + 1) * PK]))

    sums = [None] * 6
    for g in range(G):
        for first, ks, own, sib, scale in (
            (0, (0, 1), xo, xs, SCALE_IN),
            (2, (2,), co, cs, SCALE_OUT),
        ):
            plain = jnp.concatenate([own[0, 0, g], sib[0, 0, g]], axis=1)
            flip = signed(plain, jnp.concatenate([own[1, 0, g], sib[1, 0, g]], axis=1))
            for k in ks:
                for j, rhs in enumerate((plain, flip)):
                    term = (scale * nn(lhs[2 * k + j, g], rhs)).astype(BF).astype(F32)
                    at = 2 * k + j
                    sums[at] = term if sums[at] is None else sums[at] + term
    for k in range(3):
        for half in range(2):
            at = slice(half * 128, (half + 1) * 128)
            to = pl.ds(pl.multiple_of((c if half == 0 else 1 - c) * 128, 128), 128)
            mo_ref[k, :, to] = sums[2 * k][:, at].astype(BF)
            so_ref[k, :, to] = (sums[2 * k + 1][:, at] * n_ref[k, :, to].astype(F32)).astype(BF)


def grads(c, h, gu, signs, xo, xs, co, cs, noise):
    gath = pl.BlockSpec((2, 1, G, T, 128), lambda x: (0, x, 0, 0, 0))
    w = pl.BlockSpec((3, F, 256), lambda x: (0, 0, x))
    out = jax.ShapeDtypeStruct((3, F, 1024), BF)

    def whole(a):
        return pl.BlockSpec(a.shape, lambda x: (0,) * a.ndim)

    return pl.pallas_call(
        grads_body,
        grid=(4,),
        in_specs=[
            pl.BlockSpec(memory_space=pltpu.SMEM),
            whole(h),
            whole(gu),
            whole(signs),
            gath,
            gath,
            gath,
            gath,
            w,
        ],
        out_specs=[w, w],
        out_shape=[out, out],
        scratch_shapes=[pltpu.VMEM((6, G, F, T), BF)],
        name="grads",
    )(c, h, gu, signs, xo, xs, co, cs, noise)


def gather_chips(block):
    out = to_all(block, CHIP, 32).reshape(8, 4, 2, G, 24, 128)
    own = out.transpose(2, 1, 3, 0, 4, 5).reshape(2, 4, G, T, 128)
    own = lax.optimization_barrier(own)
    return own, lax.ppermute(own, "c", [(0, 1), (1, 0)])


def scatter_sum(own, sib):
    got = lax.ppermute(sib, "c", [(0, 1), (1, 0)])
    both = (own.astype(F32) + got.astype(F32)).astype(BF)
    both = both.reshape(4, G, 8, 24, 128).transpose(2, 0, 1, 3, 4).reshape(32, G * 24, 128)
    got = a2a(both, CHIP)
    return jnp.sum(got.astype(F32), axis=0).astype(BF)


def to_tokens(part):
    out = a2a(part.reshape(32, 3, 128), COLS)
    return out.transpose(1, 0, 2).reshape(3, D)


def to_sign(values):
    return (2 * values - 1).astype(BF)


def packed_signs(values):
    return pack(to_sign(values))


def on_device(
    inputs,
    weight_means,
    weight_sigmas,
    weight_noise,
    input_signs,
    output_signs,
    hidden_signs,
    result_signs,
    cotangent,
):
    c = lax.axis_index("c").reshape(1).astype(jnp.int32)
    mine = jnp.stack([inputs, to_sign(input_signs), cotangent, to_sign(result_signs)])
    mine = mine.reshape(4, 3, 32, 128).transpose(2, 0, 1, 3).reshape(32, 12, 128)
    cols = a2a(mine, COLS)
    cols = cols.reshape(G, 8, 4, 3, 128).transpose(2, 0, 1, 3, 4).reshape(4, G, 24, 128)
    signs = jnp.concatenate([packed_signs(output_signs[0]), packed_signs(output_signs[1]), packed_signs(hidden_signs)])
    cols, signs = lax.optimization_barrier((cols, signs))
    signs = to_all(signs, "dp", G)
    xo, xs = gather_chips(cols[:2])
    co, cs = gather_chips(cols[2:])
    means, perturb = prepare_weights(c, weight_means, weight_sigmas, weight_noise)
    gu = project(xo, xs, means, perturb, signs, 0, 2, SCALE_IN, "project_in")
    gu = a2a(gu, "dp")
    dh = project(co, cs, means, perturb, signs, 2, 1, SCALE_OUT, "project_cot")
    dh = a2a(dh, "dp")
    acts = pointwise(gu, dh)
    h = to_all(acts[:PK], "dp", G)
    gu_g = to_all(acts[PK:], "dp", G)
    ro, rs = back(h, signs, co, cs, means, perturb, 2, 1, SCALE_OUT, "back_result")
    result = to_tokens(scatter_sum(ro, rs))
    io, is_ = back(gu_g, signs, xo, xs, means, perturb, 0, 2, SCALE_IN, "back_input")
    input_grad = to_tokens(scatter_sum(io, is_))
    mean_grad, sigma_grad = grads(c, h, gu_g, signs, xo, xs, co, cs, weight_noise)
    return result, input_grad, mean_grad, sigma_grad


def solution(mesh):
    fine = Mesh(mesh.devices.reshape(4, 2, 4, 4, 2), ("dp", "zl", "y", "x", "c"))
    tok = P(("dp", "zl", "y", "x", "c"), None)
    ff = ("zl", "y", "x", "c")
    wide = P(None, ff, "dp")
    return jax.shard_map(
        on_device,
        mesh=fine,
        in_specs=(tok, wide, wide, wide, tok, wide, P(ff, "dp"), tok, tok),
        out_specs=(tok, tok, wide, wide),
        check_vma=False,
    )
```

time: 660 us -> 279 us (0.42)
  waiting for transfers between devices: 381 us -> 110 us
  local copies, waits for them, and re-layouts: 76.9 us -> 17.9 us
  matrix products: 41.4 us -> 0 us
  blocking collectives: 0 us -> 37.9 us
  Pallas kernels: 0 us -> 37.7 us
  other arithmetic: 41.3 us -> 4.7 us
  starting transfers between devices: 94.4 us -> 65.7 us
  between operations: 14.8 us -> 0.94 us
    all_gather x2 -> x0, waiting for transfers between devices: 207 us -> none  [sent_together(): lax.all_gather(both, axis, axis=dim, tiled=True)]
    all_to_all x12 -> x10, waiting for transfers between devices: 174 us -> 108 us  [a2a(): return lax.all_to_all(x, axes, split_axis=0, concat_axis=0, tiled=True)]
    dot_general x18 -> x0, matrix products: 41.4 us -> none  [the longest x6 18.4 us: group_sum(): jnp.einsum('fgt,gtd->gfd', left_groups, right_groups, preferred_element_t...]
    all_to_all x0 -> x2, blocking collectives: none -> 37.9 us  [a2a(): return lax.all_to_all(x, axes, split_axis=0, concat_axis=0, tiled=True)]
    pallas_call x0 -> x7, Pallas kernels: none -> 37.7 us  [the longest x2 11.2 us: back(): pl.pallas_call(lambda *refs: back_body(n, first, scale, *refs), grid=(G,)...]
    all_to_all x12 -> x10, starting transfers between devices: 94.3 us -> 65.5 us  [a2a(): return lax.all_to_all(x, axes, split_axis=0, concat_axis=0, tiled=True)]
    convert_element_type x4 -> x0, local copies, waits for them, and re-layouts: 20.7 us -> none  [the longest x1 5.2 us: on_device(): back_mean.astype(jnp.bfloat16)]
    unnamed x40 -> x14, local copies, waits for them, and re-layouts: 19.2 us -> 2.2 us
  transfers between devices with their start and end apart: 14 -> 14, of which waited for: 12 -> 11; matrix products, arithmetic and copies ran while one was open for 23% -> 4% of each run, Pallas kernels for 0% -> 11%
where the time goes in v1:
time: 279 us; the launch traced here: 275 us
  waiting for transfers between devices  110 us (39%)
  starting transfers between devices  65.7 us (24%)
  blocking collectives  37.9 us (14%)
  Pallas kernels  37.7 us (14%)
  local copies, waits for them, and re-layouts  17.9 us (6%)
  other arithmetic  4.7 us (2%)
    all_to_all x10, waiting for transfers between devices, a2a(): return lax.all_to_all(x, axes, split_axis=0, concat_axis=0, tiled=True)  108 us
    all_to_all x10, starting transfers between devices, a2a(): return lax.all_to_all(x, axes, split_axis=0, concat_axis=0, tiled=True)  65.5 us
    all_to_all x2, blocking collectives, a2a(): return lax.all_to_all(x, axes, split_axis=0, concat_axis=0, tiled=True)  37.9 us
    pallas_call x2, Pallas kernels, back(): pl.pallas_call(lambda *refs: back_body(n, first, scale, *refs), grid=(G,)...  11.2 us
    pallas_call x2, Pallas kernels, project(): pl.pallas_call(lambda *refs: project_body(n, scale, *refs), grid=(G,), in...  10.9 us
    pallas_call x1, Pallas kernels, grads(): pl.pallas_call(grads_body, grid=(4,), in_specs=[pl.BlockSpec(memory_space...  8.56 us
  transfers between devices with their start and end apart: 14, of which 11 were waited for; matrix products, arithmetic and copies ran while one was open for 4% of the time, Pallas kernels for 11%

profile of v1, /device:TPU:8, one launch (start us, length us, event | category | flops | bytes accessed | tf_op | source)
XLA Modules:
  0.0 274.8 jit_solution(15937177805869297800)
XLA Ops:
  0.6 0.9 fusion.3
  1.5 0.9 fusion.2
  2.4 0.8 copy_bitcast_fusion
  3.2 0.8 copy_bitcast_fusion.2
  4.0 0.7 copy.42
  4.7 11.3 %all-to-all-start = ((bf16[32,12,128]{2,1,0:T(8,128)(2,1)}), bf16[32,12,128]{2,1,0:T(8,128)(2,1)S(1)}, u32[]{:S(2)}, u32[]{:S(2)}) async-start(bf16[32,12,128]{2,1,0:T(8,128)(2,1)} %copy.42), calls=%async_computation | async-start | bytes 262144 | tf_op jit(solution)/shard_map/all_to_all | solution.py:23
  16.0 1.1 fusion.1
  17.1 0.1 fusion.6
  17.2 0.1 fusion.5
  17.4 0.2 concatenate.16
  17.6 9.3 %all-to-all-done = bf16[32,12,128]{2,1,0:T(8,128)(2,1)S(1)} async-done(((bf16[32,12,128]{2,1,0:T(8,128)(2,1)}), bf16[32,12,128]{2,1,0:T(8,128)(2,1)S(1)}, u32[]{:S(2)}, u32[]{:S(2)}) %all-to-all-start) | async-done | bytes 98336 | tf_op jit(solution)/shard_map/all_to_all | solution.py:23
  27.0 1.5 broadcast_in_dim.12
  28.6 6.2 %all-to-all-start.4 = ((bf16[32,2,4,24,128]{4,3,2,1,0:T(8,128)(2,1)}), bf16[32,2,4,24,128]{4,3,2,1,0:T(8,128)(2,1)S(1)}, u32[]{:S(2)}, u32[]{:S(2)}) async-start(bf16[32,2,4,24,128]{4,3,2,1,0:T(8,128)(2,1)} %broadcast_in_dim.12), calls=%async_computation.4 | async-start | bytes 3145728 | tf_op jit(solution)/shard_map/all_to_all | solution.py:23
  34.8 21.7 %all-to-all-done.4 = bf16[32,2,4,24,128]{4,3,2,1,0:T(8,128)(2,1)S(1)} async-done(((bf16[32,2,4,24,128]{4,3,2,1,0:T(8,128)(2,1)}), bf16[32,2,4,24,128]{4,3,2,1,0:T(8,128)(2,1)S(1)}, u32[]{:S(2)}, u32[]{:S(2)}) %all-to-all-start.4) | async-done | bytes 1572896 | tf_op jit(solution)/shard_map/all_to_all | solution.py:23
  56.5 1.5 broadcast_in_dim.10
  58.0 6.1 %all-to-all-start.1 = ((bf16[32,2,4,24,128]{4,3,2,1,0:T(8,128)(2,1)}), bf16[32,2,4,24,128]{4,3,2,1,0:T(8,128)(2,1)}, u32[]{:S(2)}, u32[]{:S(2)}) async-start(bf16[32,2,4,24,128]{4,3,2,1,0:T(8,128)(2,1)} %broadcast_in_dim.10), calls=%async_computation.1 | async-start | bytes 3145728 | tf_op jit(solution)/shard_map/all_to_all | solution.py:23
  64.1 0.4 copy.49
  64.5 0.1 collective-permute-start.1
  64.6 0.2 copy.47
  64.8 20.5 %all-to-all-done.1 = bf16[32,2,4,24,128]{4,3,2,1,0:T(8,128)(2,1)} async-done(((bf16[32,2,4,24,128]{4,3,2,1,0:T(8,128)(2,1)}), bf16[32,2,4,24,128]{4,3,2,1,0:T(8,128)(2,1)}, u32[]{:S(2)}, u32[]{:S(2)}) %all-to-all-start.1) | async-done | bytes 1572896 | tf_op jit(solution)/shard_map/all_to_all | solution.py:23
  85.3 1.1 broadcast_in_dim.11
  86.4 3.5 %all-to-all-start.2 = ((bf16[4,1008,128]{2,1,0:T(8,128)(2,1)}), bf16[4,1008,128]{2,1,0:T(8,128)(2,1)S(1)}, u32[]{:S(2)}, u32[]{:S(2)}) async-start(bf16[4,1008,128]{2,1,0:T(8,128)(2,1)} %broadcast_in_dim.11), calls=%async_computation.2 | async-start | bytes 2064384 | tf_op jit(solution)/shard_map/all_to_all | solution.py:23
  89.9 3.0 %copy.46 = bf16[2,4,4,8,24,128]{5,4,3,2,1,0:T(8,128)(2,1)} copy(bf16[2,4,4,8,24,128]{5,4,2,0,1,3:T(8,128)(2,1)} %bitcast.8) | data formatting | bytes 3145728 | tf_op jit(solution)/shard_map/transpose | solution.py:227
  92.9 0.0 collective-permute-start
  92.9 4.9 %prepare_weights.1 = (bf16[3,224,1024]{2,1,0:T(8,128)(2,1)}, bf16[3,224,1024]{2,1,0:T(8,128)(2,1)}) custom-call(s32[1]{0:T(128)} %bitcast.10.c_ref, bf16[3,224,1024]{2,1,0:T(8,128)(2,1)} %m_ref.1, bf16[3,224,1024]{2,1,0:T(8,128)(2,1)} %s_ref.1, bf16[3,224,1024]{2,1,0:T(8,128)(2,1)} %n_ref.3), custom_call_target="tpu_custom_call" | custom-call | tf_op jit(solution)/shard_map/prepare_weights/pallas_call | solution.py:76
  97.8 9.3 %all-to-all-done.2.refs_4_.refs_1_.s_ref = bf16[4,1008,128]{2,1,0:T(8,128)(2,1)S(1)} async-done(((bf16[4,1008,128]{2,1,0:T(8,128)(2,1)}), bf16[4,1008,128]{2,1,0:T(8,128)(2,1)S(1)}, u32[]{:S(2)}, u32[]{:S(2)}) %all-to-all-start.2) | async-done | bytes 1032224 | tf_op jit(solution)/shard_map/all_to_all | solution.py:23
  107.2 0.0 collective-permute-done.1.refs_1_.refs_3_.cs
  107.2 1.0 copy-done
  108.1 4.9 %project_cot.1 = bf16[4,336,128]{2,1,0:T(8,128)(2,1)} custom-call(bf16[2,4,4,192,128]{4,3,2,1,0:T(8,128)(2,1)} %bitcast.53, bf16[2,4,4,192,128]{4,3,2,1,0:T(8,128)(2,1)} %collective-permute-done.1.refs_1_.refs_3_.cs, bf16[3,224,1024]{2,1,0:T(8,128)(2,1)} %get-tuple-element.15.refs_2_.refs_4_, bf16[3,224,1024]{2,1,0:T(8,128)(2,1)} %get-tuple-element.16.refs_3_.refs_5_, ...), custom_call_target="tpu_custom_call" | custom-call | tf_op jit(solution)/shard_map/project_cot/pallas_call | solution.py:102
  113.0 10.6 %all-to-all-start.5 = ((bf16[4,336,128]{2,1,0:T(8,128)(2,1)}), bf16[4,336,128]{2,1,0:T(8,128)(2,1)S(1)}, u32[]{:S(2)}, u32[]{:S(2)}) async-start(bf16[4,336,128]{2,1,0:T(8,128)(2,1)} %project_cot.1), calls=%async_computation.5 | async-start | bytes 688128 | tf_op jit(solution)/shard_map/all_to_all | solution.py:23
  123.6 0.0 collective-permute-done.refs_1_.refs_3_.xs
  123.6 6.0 %project_in.1 = bf16[4,672,128]{2,1,0:T(8,128)(2,1)} custom-call(bf16[2,4,4,192,128]{4,3,2,1,0:T(8,128)(2,1)} %bitcast.9.refs_0_.refs_2_.xo, bf16[2,4,4,192,128]{4,3,2,1,0:T(8,128)(2,1)} %collective-permute-done.refs_1_.refs_3_.xs, bf16[3,224,1024]{2,1,0:T(8,128)(2,1)} %get-tuple-element.15.refs_2_.refs_4_, ...), custom_call_target="tpu_custom_call" | custom-call | tf_op jit(solution)/shard_map/project_in/pallas_call | solution.py:102
  129.6 5.5 %all-to-all-done.5.dh_ref = bf16[4,336,128]{2,1,0:T(8,128)(2,1)S(1)} async-done(((bf16[4,336,128]{2,1,0:T(8,128)(2,1)}), bf16[4,336,128]{2,1,0:T(8,128)(2,1)S(1)}, u32[]{:S(2)}, u32[]{:S(2)}) %all-to-all-start.5) | async-done | bytes 344096 | tf_op jit(solution)/shard_map/all_to_all | solution.py:23
  135.2 21.5 %all_to_all.60.gu_ref = bf16[4,672,128]{2,1,0:T(8,128)(2,1)} all-to-all(bf16[4,672,128]{2,1,0:T(8,128)(2,1)} %project_in.1), channel_id=1, replica_groups=mesh['dp'=4,'zl'=2,'y'=4,'x'=4,'c'=2] {'dp'}, dimensions={0} | all-to-all | bytes 1376256 | tf_op jit(solution)/shard_map/all_to_all | solution.py:23
  156.7 2.1 pointwise.1
  158.7 0.9 slice.69
  159.7 16.4 %all_to_all.61.refs_0_.h_ref = bf16[4,336,128]{2,1,0:T(8,128)(2,1)} all-to-all(bf16[4,336,128]{2,1,0:T(8,128)(2,1)S(1)} %broadcast_in_dim.13), channel_id=1, replica_groups=mesh['dp'=4,'zl'=2,'y'=4,'x'=4,'c'=2] {'dp'}, dimensions={0} | all-to-all | bytes 688128 | tf_op jit(solution)/shard_map/all_to_all | solution.py:23
  176.1 5.1 %back_result.1 = (bf16[4,4,192,128]{3,2,1,0:T(8,128)(2,1)}, bf16[4,4,192,128]{3,2,1,0:T(8,128)(2,1)}) custom-call(bf16[4,336,128]{2,1,0:T(8,128)(2,1)} %all_to_all.61.refs_0_.h_ref, bf16[4,1008,128]{2,1,0:T(8,128)(2,1)} %copy-done, bf16[2,4,4,192,128]{4,3,2,1,0:T(8,128)(2,1)} %bitcast.54, ...), custom_call_target="tpu_custom_call" | custom-call | tf_op jit(solution)/shard_map/back_result/pallas_call | solution.py:154
  181.2 0.1 collective-permute-start.2
  181.3 0.9 broadcast_in_dim.14
  182.2 3.5 %all-to-all-start.9 = ((bf16[4,672,128]{2,1,0:T(8,128)(2,1)}), bf16[4,672,128]{2,1,0:T(8,128)(2,1)S(1)}, u32[]{:S(2)}, u32[]{:S(2)}) async-start(bf16[4,672,128]{2,1,0:T(8,128)(2,1)} %broadcast_in_dim.14), calls=%async_computation.9 | async-start | bytes 1376256 | tf_op jit(solution)/shard_map/all_to_all | solution.py:23
  185.7 0.0 collective-permute-done.2
  185.8 0.2 add_convert_fusion.1
  186.0 1.1 copy.50
  187.0 16.4 %all-to-all-done.9.refs_0_.gu_ref = bf16[4,672,128]{2,1,0:T(8,128)(2,1)S(1)} async-done(((bf16[4,672,128]{2,1,0:T(8,128)(2,1)}), bf16[4,672,128]{2,1,0:T(8,128)(2,1)S(1)}, u32[]{:S(2)}, u32[]{:S(2)}) %all-to-all-start.9) | async-done | bytes 688160 | tf_op jit(solution)/shard_map/all_to_all | solution.py:23
  203.4 10.2 %all-to-all-start.7 = ((bf16[32,96,128]{2,1,0:T(8,128)(2,1)}), bf16[32,96,128]{2,1,0:T(8,128)(2,1)S(1)}, u32[]{:S(2)}, u32[]{:S(2)}) async-start(bf16[32,96,128]{2,1,0:T(8,128)(2,1)} %bitcast.16), calls=%async_computation.7 | async-start | bytes 1572864 | tf_op jit(solution)/shard_map/all_to_all | solution.py:23
  213.6 6.1 %back_input.1 = (bf16[4,4,192,128]{3,2,1,0:T(8,128)(2,1)}, bf16[4,4,192,128]{3,2,1,0:T(8,128)(2,1)}) custom-call(bf16[4,672,128]{2,1,0:T(8,128)(2,1)} %copy-done.2, bf16[4,1008,128]{2,1,0:T(8,128)(2,1)} %copy-done, bf16[2,4,4,192,128]{4,3,2,1,0:T(8,128)(2,1)} %bitcast.9.refs_0_.refs_2_.xo, ...), custom_call_target="tpu_custom_call" | custom-call | tf_op jit(solution)/shard_map/back_input/pallas_call | solution.py:154
  219.7 2.5 collective-permute-done.3
  222.2 1.3 add_convert_fusion
  223.6 1.0 copy.51
  224.6 1.9 all-to-all-done.7
  226.5 6.4 %all-to-all-start.10 = ((bf16[32,96,128]{2,1,0:T(8,128)(2,1)}), bf16[32,96,128]{2,1,0:T(8,128)(2,1)S(1)}, u32[]{:S(2)}, u32[]{:S(2)}) async-start(bf16[32,96,128]{2,1,0:T(8,128)(2,1)} %bitcast.21), calls=%async_computation.10 | async-start | bytes 1572864 | tf_op jit(solution)/shard_map/all_to_all | solution.py:23
  232.9 0.1 reduce_sum.24
  233.0 0.6 reshape.90
  233.7 12.3 %all-to-all-done.10 = bf16[32,96,128]{2,1,0:T(8,128)(2,1)S(1)} async-done(((bf16[32,96,128]{2,1,0:T(8,128)(2,1)}), bf16[32,96,128]{2,1,0:T(8,128)(2,1)S(1)}, u32[]{:S(2)}, u32[]{:S(2)}) %all-to-all-start.10) | async-done | bytes 786464 | tf_op jit(solution)/shard_map/all_to_all | solution.py:23
  246.0 3.9 %all-to-all-start.8 = ((bf16[32,3,128]{2,1,0:T(4,128)(2,1)}), bf16[32,3,128]{2,1,0:T(4,128)(2,1)S(1)}, u32[]{:S(2)}, u32[]{:S(2)}) async-start(bf16[32,3,128]{2,1,0:T(4,128)(2,1)} %reshape.90), calls=%async_computation.8 | async-start | bytes 65536 | tf_op jit(solution)/shard_map/all_to_all | solution.py:23
  249.8 0.1 reduce_sum.25
  249.9 0.6 reshape.94
  250.6 9.2 %all-to-all-done.8 = bf16[32,3,128]{2,1,0:T(4,128)(2,1)S(1)} async-done(((bf16[32,3,128]{2,1,0:T(4,128)(2,1)}), bf16[32,3,128]{2,1,0:T(4,128)(2,1)S(1)}, u32[]{:S(2)}, u32[]{:S(2)}) %all-to-all-start.8) | async-done | bytes 24608 | tf_op jit(solution)/shard_map/all_to_all | solution.py:23
  259.8 3.9 %all-to-all-start.11 = ((bf16[32,3,128]{2,1,0:T(4,128)(2,1)}), bf16[32,3,128]{2,1,0:T(4,128)(2,1)S(1)}, u32[]{:S(2)}, u32[]{:S(2)}) async-start(bf16[32,3,128]{2,1,0:T(4,128)(2,1)} %reshape.94), calls=%async_computation.11 | async-start | bytes 65536 | tf_op jit(solution)/shard_map/all_to_all | solution.py:23
  263.7 8.6 %grads.1 = (bf16[3,224,1024]{2,1,0:T(8,128)(2,1)}, bf16[3,224,1024]{2,1,0:T(8,128)(2,1)}) custom-call(s32[1]{0:T(128)} %bitcast.10.c_ref, bf16[4,336,128]{2,1,0:T(8,128)(2,1)} %all_to_all.61.refs_0_.h_ref, bf16[4,672,128]{2,1,0:T(8,128)(2,1)} %copy-done.2, bf16[4,1008,128]{2,1,0:T(8,128)(2,1)} %copy-done, ...), custom_call_target="tpu_custom_call" | custom-call | tf_op jit(solution)/shard_map/grads/pallas_call | solution.py:204
  272.2 1.3 all-to-all-done.11
  273.6 0.6 copy.62
  274.2 0.6 copy.63
  (28 shorter events, 0.3 us)
Async XLA Ops:
  0.6 16.5 %copy-start.5 = (s32[224,192]{0,1:T(8,128)S(1)}, s32[224,192]{0,1:T(8,128)}, u32[]{:S(2)}) copy-start(s32[224,192]{0,1:T(8,128)} %param.15) | copy-start | bytes 516100
  4.7 22.2 %all-to-all-start = ((bf16[32,12,128]{2,1,0:T(8,128)(2,1)}), bf16[32,12,128]{2,1,0:T(8,128)(2,1)S(1)}, u32[]{:S(2)}, u32[]{:S(2)}) async-start(bf16[32,12,128]{2,1,0:T(8,128)(2,1)} %copy.42), calls=%async_computation | async-start | bytes 262144 | tf_op jit(solution)/shard_map/all_to_all | solution.py:23
  28.6 27.9 %all-to-all-start.4 = ((bf16[32,2,4,24,128]{4,3,2,1,0:T(8,128)(2,1)}), bf16[32,2,4,24,128]{4,3,2,1,0:T(8,128)(2,1)S(1)}, u32[]{:S(2)}, u32[]{:S(2)}) async-start(bf16[32,2,4,24,128]{4,3,2,1,0:T(8,128)(2,1)} %broadcast_in_dim.12), calls=%async_computation.4 | async-start | bytes 3145728 | tf_op jit(solution)/shard_map/all_to_all | solution.py:23
  58.0 27.3 %all-to-all-start.1 = ((bf16[32,2,4,24,128]{4,3,2,1,0:T(8,128)(2,1)}), bf16[32,2,4,24,128]{4,3,2,1,0:T(8,128)(2,1)}, u32[]{:S(2)}, u32[]{:S(2)}) async-start(bf16[32,2,4,24,128]{4,3,2,1,0:T(8,128)(2,1)} %broadcast_in_dim.10), calls=%async_computation.1 | async-start | bytes 3145728 | tf_op jit(solution)/shard_map/all_to_all | solution.py:23
  64.5 21.9 %copy-start.1 = (bf16[2,4,4,8,24,128]{5,4,3,2,1,0:T(8,128)(2,1)}, bf16[2,4,4,8,24,128]{5,4,3,2,1,0:T(8,128)(2,1)S(1)}, u32[]{:S(2)}) copy-start(bf16[2,4,4,8,24,128]{5,4,3,2,1,0:T(8,128)(2,1)S(1)} %copy.49) | copy-start | bytes 4718596
  64.5 42.6 %collective-permute-start.1 = (bf16[2,4,4,192,128]{4,3,2,1,0:T(8,128)(2,1)S(1)}, bf16[2,4,4,192,128]{4,3,2,1,0:T(8,128)(2,1)}, u32[]{:S(2)}, u32[]{:S(2)}) collective-permute-start(bf16[2,4,4,192,128]{4,3,2,1,0:T(8,128)(2,1)S(1)} %bitcast.52), channel_id=1, source_target_pairs={{0,1},{1,0},{2,3},{3,2},{4,5},{5,4},{6,7},{7,6},{8,9},{9,8},{10,11... | collective-permute-start | bytes 4718600 | tf_op jit(solution)/shard_map/ppermute | solution.py:229
  86.4 20.8 %all-to-all-start.2 = ((bf16[4,1008,128]{2,1,0:T(8,128)(2,1)}), bf16[4,1008,128]{2,1,0:T(8,128)(2,1)S(1)}, u32[]{:S(2)}, u32[]{:S(2)}) async-start(bf16[4,1008,128]{2,1,0:T(8,128)(2,1)} %broadcast_in_dim.11), calls=%async_computation.2 | async-start | bytes 2064384 | tf_op jit(solution)/shard_map/all_to_all | solution.py:23
  92.9 30.7 %collective-permute-start = (bf16[2,4,4,192,128]{4,3,2,1,0:T(8,128)(2,1)}, bf16[2,4,4,192,128]{4,3,2,1,0:T(8,128)(2,1)}, u32[]{:S(2)}, u32[]{:S(2)}) collective-permute-start(bf16[2,4,4,192,128]{4,3,2,1,0:T(8,128)(2,1)} %bitcast.9.refs_0_.refs_2_.xo), channel_id=1, source_target_pairs={{0,1},{1,0},{2,3},{3,2},{4,5},{5,4},{6,7},{7,6},{8,9},{9,8},{10,11... | collective-permute-start | bytes 4718600 | tf_op jit(solution)/shard_map/ppermute | solution.py:229
  107.2 1.0 copy-start
  113.0 22.2 %all-to-all-start.5 = ((bf16[4,336,128]{2,1,0:T(8,128)(2,1)}), bf16[4,336,128]{2,1,0:T(8,128)(2,1)S(1)}, u32[]{:S(2)}, u32[]{:S(2)}) async-start(bf16[4,336,128]{2,1,0:T(8,128)(2,1)} %project_cot.1), calls=%async_computation.5 | async-start | bytes 688128 | tf_op jit(solution)/shard_map/all_to_all | solution.py:23
  135.2 21.5 %copy-start.3 = (bf16[4,336,128]{2,1,0:T(8,128)(2,1)}, bf16[4,336,128]{2,1,0:T(8,128)(2,1)S(1)}, u32[]{:S(2)}) copy-start(bf16[4,336,128]{2,1,0:T(8,128)(2,1)S(1)} %all-to-all-done.5.dh_ref) | copy-start | bytes 1032196
  176.1 5.2 %slice-start = ((bf16[1008,128]{1,0:T(8,128)(2,1)}), bf16[672,128]{1,0:T(8,128)(2,1)S(1)}, s32[]{:S(2)}) async-start(bf16[1008,128]{1,0:T(8,128)(2,1)} %pointwise.1), calls=%async_computation.12 | async-start | bytes 344064 | tf_op jit(solution)/shard_map/slice | solution.py:281
  181.2 4.6 %copy-start.4 = (bf16[4,4,192,128]{3,2,1,0:T(8,128)(2,1)S(1)}, bf16[4,4,192,128]{3,2,1,0:T(8,128)(2,1)}, u32[]{:S(2)}) copy-start(bf16[4,4,192,128]{3,2,1,0:T(8,128)(2,1)} %get-tuple-element.18) | copy-start | bytes 2359300
  181.2 4.5 %collective-permute-start.2 = (bf16[4,4,192,128]{3,2,1,0:T(8,128)(2,1)}, bf16[4,4,192,128]{3,2,1,0:T(8,128)(2,1)S(1)}, u32[]{:S(2)}, u32[]{:S(2)}) collective-permute-start(bf16[4,4,192,128]{3,2,1,0:T(8,128)(2,1)} %get-tuple-element.19), channel_id=1, source_target_pairs={{0,1},{1,0},{2,3},{3,2},{4,5},{5,4},{6,7},{7,6},{8,9},{9,8},{10,11... | collective-permute-start | bytes 2359304 | tf_op jit(solution)/shard_map/ppermute | solution.py:233
  182.2 21.2 %all-to-all-start.9 = ((bf16[4,672,128]{2,1,0:T(8,128)(2,1)}), bf16[4,672,128]{2,1,0:T(8,128)(2,1)S(1)}, u32[]{:S(2)}, u32[]{:S(2)}) async-start(bf16[4,672,128]{2,1,0:T(8,128)(2,1)} %broadcast_in_dim.14), calls=%async_computation.9 | async-start | bytes 1376256 | tf_op jit(solution)/shard_map/all_to_all | solution.py:23
  203.4 10.2 %copy-start.2 = (bf16[4,672,128]{2,1,0:T(8,128)(2,1)}, bf16[4,672,128]{2,1,0:T(8,128)(2,1)S(1)}, u32[]{:S(2)}) copy-start(bf16[4,672,128]{2,1,0:T(8,128)(2,1)S(1)} %all-to-all-done.9.refs_0_.gu_ref) | copy-start | bytes 2064388
  203.4 23.0 %all-to-all-start.7 = ((bf16[32,96,128]{2,1,0:T(8,128)(2,1)}), bf16[32,96,128]{2,1,0:T(8,128)(2,1)S(1)}, u32[]{:S(2)}, u32[]{:S(2)}) async-start(bf16[32,96,128]{2,1,0:T(8,128)(2,1)} %bitcast.16), calls=%async_computation.7 | async-start | bytes 1572864 | tf_op jit(solution)/shard_map/all_to_all | solution.py:23
  219.7 2.5 collective-permute-start.3
  226.5 19.5 %all-to-all-start.10 = ((bf16[32,96,128]{2,1,0:T(8,128)(2,1)}), bf16[32,96,128]{2,1,0:T(8,128)(2,1)S(1)}, u32[]{:S(2)}, u32[]{:S(2)}) async-start(bf16[32,96,128]{2,1,0:T(8,128)(2,1)} %bitcast.21), calls=%async_computation.10 | async-start | bytes 1572864 | tf_op jit(solution)/shard_map/all_to_all | solution.py:23
  246.0 13.8 %all-to-all-start.8 = ((bf16[32,3,128]{2,1,0:T(4,128)(2,1)}), bf16[32,3,128]{2,1,0:T(4,128)(2,1)S(1)}, u32[]{:S(2)}, u32[]{:S(2)}) async-start(bf16[32,3,128]{2,1,0:T(4,128)(2,1)} %reshape.90), calls=%async_computation.8 | async-start | bytes 65536 | tf_op jit(solution)/shard_map/all_to_all | solution.py:23
  259.8 13.8 %all-to-all-start.11 = ((bf16[32,3,128]{2,1,0:T(4,128)(2,1)}), bf16[32,3,128]{2,1,0:T(4,128)(2,1)S(1)}, u32[]{:S(2)}, u32[]{:S(2)}) async-start(bf16[32,3,128]{2,1,0:T(4,128)(2,1)} %reshape.94), calls=%async_computation.11 | async-start | bytes 65536 | tf_op jit(solution)/shard_map/all_to_all | solution.py:23
